TPU v7x, 32 devices: a whole 2x2x4 slice. The times are simulated.
32 devices in a mesh: groups: 2 (over y), ctx: 4 (over z), tp: 4 (over x, core).
Axes of the slice: x: 2, y: 2, z: 4, core: 2. Of those that a mesh axis runs over, the one named last changes fastest.
Arguments:
- queries: bfloat16 [2048, 5120], P(('groups', 'ctx'), 'tp'), parts along dimension 0, may hold values from -16 to 16
- keys: bfloat16 [2048, 1024], P(('groups', 'ctx'), 'tp'), parts along dimension 0, may hold values from -16 to 16
- values: bfloat16 [2048, 1024], P(('groups', 'ctx'), 'tp'), parts along dimension 0, may hold values from -6 to 6
- positions: int32 [2048], P('groups'), parts along dimension 0, may hold values from 0 to 1023, as said below
- out_weight: bfloat16 [5120, 5120], P('tp', 'ctx'), may hold values from -0.59765625 to 0.59765625
Outputs:
- mixed: bfloat16 [2048, 5120], P(('groups', 'ctx'), 'tp'), parts along dimension 0
There are 2 independent parts, one for each index of `groups`. A program takes and returns all parts, laid end to end along the dimension named above; an argument that names none is the same for every part. Nothing has to cross between parts.
Inputs may be any that keep to these rules, and one draw needn't show every extreme that they name: positions is a permutation of all positions made of 8 aligned runs of 128 consecutive positions, each run increasing.
All inputs are finite; a program needn't handle non-finite values.
Results may differ from a plain program's by a relative error of at most 0.0095.
Values may be sent and summed in bfloat16 or wider, within the bound.
No kernel may reach another device: no remote copies, remote signals or barrier semaphores. Data moves between devices by JAX's collectives and lax.ppermute only.
A program may use at most 64 MiB of HBM per device.

v0:
```python
import math

import jax
import jax.numpy as jnp
from jax import lax
from jax.sharding import PartitionSpec as P

QUERY_HEADS = 40
KEY_VALUE_HEADS = 8
HEAD_SIZE = 128


def local(queries, keys, values, positions, out_weight):
    tok = queries.shape[0]
    kv_heads = keys.shape[1] // HEAD_SIZE
    query_group = QUERY_HEADS // KEY_VALUE_HEADS
    scale = HEAD_SIZE ** (-0.5)
    ctx_index = lax.axis_index("ctx")
    query_pos = lax.dynamic_slice_in_dim(positions, ctx_index * tok, tok)
    query_four = queries.reshape(tok, kv_heads, query_group, HEAD_SIZE)

    def attend(carry, key_block, value_block, key_pos):
        top, total, accum = carry
        count = key_block.shape[0]
        key_three = key_block.reshape(count, kv_heads, HEAD_SIZE)
        value_three = value_block.reshape(count, kv_heads, HEAD_SIZE)
        scores = (
            jnp.einsum("tgjd,kgd->gjtk", query_four, key_three, preferred_element_type=jnp.float32)
            * scale
        )
        keep = key_pos[None, :] <= query_pos[:, None]
        scores = jnp.where(keep, scores, -1e30)
        new_top = jnp.maximum(top, jnp.max(scores, axis=-1))
        factor = jnp.exp(top - new_top)
        expo = jnp.where(keep, jnp.exp(scores - new_top[..., None]), 0.0)
        total = total * factor + jnp.sum(expo, axis=-1)
        weights = expo.astype(jnp.bfloat16)
        accum = accum * factor[..., None] + jnp.einsum(
            "gjtk,kgd->gjtd", weights, value_three, preferred_element_type=jnp.float32
        )
        return (new_top, total, accum)

    start_top = jnp.full((kv_heads, query_group, tok), -1e30, jnp.float32)
    start_total = jnp.zeros((kv_heads, query_group, tok), jnp.float32)
    start_accum = jnp.zeros((kv_heads, query_group, tok, HEAD_SIZE), jnp.float32)
    key_piece = lax.all_gather(keys, "ctx", axis=0, tiled=True)
    value_piece = lax.all_gather(values, "ctx", axis=0, tiled=True)
    rows = key_piece.shape[0]
    width = math.gcd(rows, 512)

    def step(index, state):
        offset = index * width
        key_block = lax.dynamic_slice_in_dim(key_piece, offset, width, 0)
        value_block = lax.dynamic_slice_in_dim(value_piece, offset, width, 0)
        key_pos = lax.dynamic_slice_in_dim(positions, offset, width, 0)
        return attend(state, key_block, value_block, key_pos)

    top, total, accum = lax.fori_loop(0, rows // width, step, (start_top, start_total, start_accum))
    attended = (
        (accum / total[..., None])
        .transpose(2, 0, 1, 3)
        .reshape(tok, kv_heads * query_group * HEAD_SIZE)
        .astype(jnp.bfloat16)
    )
    partial_value = jnp.dot(
        attended,
        lax.all_gather(out_weight, "ctx", axis=1, tiled=True),
        preferred_element_type=jnp.float32,
    )
    summed = lax.psum_scatter(
        partial_value.astype(jnp.bfloat16), "tp", scatter_dimension=1, tiled=True
    )
    return summed


def solution(mesh):
    return jax.shard_map(
        local,
        mesh=mesh,
        in_specs=(
            P(("groups", "ctx"), "tp"),
            P(("groups", "ctx"), "tp"),
            P(("groups", "ctx"), "tp"),
            P("groups"),
            P("tp", "ctx"),
        ),
        out_specs=P(("groups", "ctx"), "tp"),
        check_vma=False,
    )
```

profile of v0, /device:TPU:0, one launch (start us, length us, event | category | flops | bytes accessed | tf_op | source)
XLA Modules:
  0.0 296.8 jit_solution(16109879064267613819)
XLA Ops:
  6.5 0.0 all-gather.2.cloned.1.call-start
  6.5 0.7 all-gather.2.cloned.1.call-update
  7.3 0.0 reduce-scatter.2.cloned.1.call-start
  7.3 1.3 copy.11
  8.7 0.3 copy.13
  9.0 0.0 copy-done.1
  9.0 0.1 copy.12
  9.1 0.0 copy-done.2
  9.1 0.1 copy.10
  9.2 0.0 copy-done.3
  9.2 0.1 dynamic_slice.24
  9.3 19.1 %all_gather.10 = bf16[1024,256]{0,1:T(8,128)(2,1)S(1)} all-gather(bf16[256,256]{0,1:T(8,128)(2,1)S(1)} %copy.12), channel_id=1, replica_groups=mesh['groups'=2,'ctx'=4,'tp'=4] {'ctx'}, dimensions={0}, use_global_device_ids=true | all-gather | bytes 655360 | tf_op jit(solution)/shard_map/all_gather | solution.py:47
  28.4 30.9 %all_gather.9 = bf16[1024,256]{0,1:T(8,128)(2,1)S(1)} all-gather(bf16[256,256]{0,1:T(8,128)(2,1)S(1)} %copy.10), channel_id=1, replica_groups=mesh['groups'=2,'ctx'=4,'tp'=4] {'ctx'}, dimensions={0}, use_global_device_ids=true | all-gather | bytes 655360 | tf_op jit(solution)/shard_map/all_gather | solution.py:46
  59.3 19.9 %while.18 = (s32[]{:T(128)}, f32[2,5,256]{2,1,0:T(8,128)S(1)}, f32[2,5,256]{2,1,0:T(8,128)S(1)}, f32[2,5,256,128]{3,2,1,0:T(8,128)S(1)}, s32[1024]{0:T(1024)S(1)...) while((s32[]{:T(128)}, f32[2,5,256]{2,1,0:T(8,128)S(1)}, ...), condition=%wide.region_3.4_spmd.clone, body=%wide.region_0.3_spmd.clone.sunk | while | flops 689254912 | bytes 42245336 | solution.py:58
  59.3 0.1 dynamic_slice.33
  59.3 0.1 broadcast_compare_fusion.2
  59.6 3.3 %fusion.30 = (f32[2,5,256]{2,1,0:T(8,128)S(1)}, f32[2,512,256,5]{2,1,3,0:T(8,128)}) fusion(pred[256,512]{0,1:T(8,128)(4,1)S(1)} %broadcast_compare_fusion.2, bf16[512,2,128,1]{0,2,3,1:T(8,128)(2,1)S(1)} %bitcast.48, bf16[256,2,5,128]{3,0,2,1:T(8,128)(2,1)S(1)} %get-tuple-element.325), kind=kOutput, calls=%fused_computation.2.clone.1 | convolution fusion | flops 339473920 | bytes 6301696 | tf_op jit(solution)/shard_map/while/body/eval_jaxpr/tgjd,kgd->gjtk/dot_general | solution.py:28
  62.9 4.0 %fusion.31 = f32[2,5,256]{2,1,0:T(8,128)S(1)} fusion(f32[2,512,256,5]{2,1,3,0:T(8,128)} %get-tuple-element.288, f32[2,5,256]{2,1,0:T(8,128)S(1)} %select_maximum_fusion.2, pred[256,512]{0,1:T(8,128)(4,1)S(1)} %broadcast_compare_fusion.2), kind=kLoop, calls=%fused_computation.4.clone.1 | loop fusion | flops 6551040 | bytes 5394432 | tf_op jit(solution)/shard_map/while/body/eval_jaxpr/reduce_sum | solution.py:36
  66.9 0.2 copy-done
  67.1 2.2 fusion.33
  69.3 0.1 dynamic_slice.33
  69.4 0.1 broadcast_compare_fusion.2
  69.6 3.3 %fusion.30 = (f32[2,5,256]{2,1,0:T(8,128)S(1)}, f32[2,512,256,5]{2,1,3,0:T(8,128)}) fusion(pred[256,512]{0,1:T(8,128)(4,1)S(1)} %broadcast_compare_fusion.2, bf16[512,2,128,1]{0,2,3,1:T(8,128)(2,1)S(1)} %bitcast.48, bf16[256,2,5,128]{3,0,2,1:T(8,128)(2,1)S(1)} %get-tuple-element.325), kind=kOutput, calls=%fused_computation.2.clone.1 | convolution fusion | flops 339473920 | bytes 6301696 | tf_op jit(solution)/shard_map/while/body/eval_jaxpr/tgjd,kgd->gjtk/dot_general | solution.py:28
  72.9 3.9 %fusion.31 = f32[2,5,256]{2,1,0:T(8,128)S(1)} fusion(f32[2,512,256,5]{2,1,3,0:T(8,128)} %get-tuple-element.288, f32[2,5,256]{2,1,0:T(8,128)S(1)} %select_maximum_fusion.2, pred[256,512]{0,1:T(8,128)(4,1)S(1)} %broadcast_compare_fusion.2), kind=kLoop, calls=%fused_computation.4.clone.1 | loop fusion | flops 6551040 | bytes 5394432 | tf_op jit(solution)/shard_map/while/body/eval_jaxpr/reduce_sum | solution.py:36
  76.8 0.1 copy-done
  77.0 2.2 fusion.33
  79.2 0.4 copy.14
  79.6 0.1 divide_convert_fusion
  79.8 167.2 %all-gather.2.cloned.1.call-done = bf16[1280,5120]{1,0:T(8,128)(2,1)} async-done(((bf16[1280,1280]{1,0:T(8,128)(2,1)}), bf16[1280,5120]{1,0:T(8,128)(2,1)}) %all-gather.2.cloned.1.call-update) | async-done | bytes 13107216 | tf_op jit(solution)/shard_map/all_gather | solution.py:67
  247.0 9.7 %convolution_convert_fusion = bf16[256,5120]{1,0:T(8,128)(2,1)} fusion(bf16[256,1280]{0,1:T(8,128)(2,1)S(1)} %bitcast.50, bf16[1280,5120]{1,0:T(8,128)(2,1)} %all-gather.2.cloned.1.call-done), kind=kOutput, calls=%fused_computation.19 | convolution fusion | flops 3356753920 | bytes 16384000 | tf_op jit(solution)/shard_map/dot_general | solution.py:65
  256.7 0.0 reduce-scatter.2.cloned.1.call-update
  256.7 33.3 %reduce-scatter.2.cloned.1.call-done = bf16[256,1280]{1,0:T(8,128)(2,1)} async-done(((bf16[256,5120]{1,0:T(8,128)(2,1)}), bf16[256,1280]{1,0:T(8,128)(2,1)}) %reduce-scatter.2.cloned.1.call-update) | async-done | bytes 655376 | tf_op jit(solution)/shard_map/reduce_scatter | solution.py:70
  (16 shorter events, 0.2 us)
Async XLA Ops:
  6.5 2.5 copy-start.1
  6.5 2.6 copy-start.2
  6.5 2.7 copy-start.3
  6.5 240.4 %all-gather.2.cloned.1.call-start = ((), (), s32[]{:S(2)}) async-start(), calls=%async_computation.1 | async-start | bytes 16384000 | tf_op jit(solution)/shard_map/all_gather | solution.py:67
  7.3 282.7 %reduce-scatter.2.cloned.1.call-start = ((), (), s32[]{:S(2)}) async-start(), calls=%async_computation.2 | async-start | bytes 3276800 | tf_op jit(solution)/shard_map/reduce_scatter | solution.py:70
  62.9 4.2 %copy-start = (f32[2,512,256,5]{2,1,3,0:T(8,128)S(1)}, f32[2,512,256,5]{2,1,3,0:T(8,128)}, u32[]{:S(2)}) copy-start(f32[2,512,256,5]{2,1,3,0:T(8,128)} %get-tuple-element.288) | copy-start | bytes 15728644 | tf_op jit(solution)/shard_map/while
  72.9 4.0 %copy-start = (f32[2,512,256,5]{2,1,3,0:T(8,128)S(1)}, f32[2,512,256,5]{2,1,3,0:T(8,128)}, u32[]{:S(2)}) copy-start(f32[2,512,256,5]{2,1,3,0:T(8,128)} %get-tuple-element.288) | copy-start | bytes 15728644 | tf_op jit(solution)/shard_map/while
Sparse Core Ops, SparseCore 0:
  8.9 238.0 all-gather.1
  256.8 33.1 reduce-scatter.1
where the time goes:
time: 297 us
  waiting for transfers between devices  201 us (68%)
  blocking collectives  49.9 us (17%)
  matrix products  20.8 us (7%)
  between operations  13.5 us (5%)
  other arithmetic  8.32 us (3%)
    all_gather x1, waiting for transfers between devices, local(): lax.all_gather(out_weight, 'ctx', axis=1, tiled=True)  167 us
    reduce_scatter x1, waiting for transfers between devices, local(): lax.psum_scatter(partial_value.astype(jnp.bfloat16), 'tp', scatter_dimens...  33.3 us
    all_gather x1, blocking collectives, local(): key_piece = lax.all_gather(keys, 'ctx', axis=0, tiled=True)  30.9 us
    all_gather x1, blocking collectives, local(): value_piece = lax.all_gather(values, 'ctx', axis=0, tiled=True)  19.1 us
    dot_general x1, matrix products, local(): jnp.dot(attended, lax.all_gather(out_weight, 'ctx', axis=1, tiled=True),...  9.69 us
    reduce_sum x2, other arithmetic, attend(): total = total * factor + jnp.sum(expo, axis=-1)  7.85 us
    dot_general x2, matrix products, attend(): jnp.einsum('tgjd,kgd->gjtk', query_four, key_three, preferred_element_typ...  6.64 us
  transfers between devices with their start and end apart: 2, of which 2 were waited for; matrix products, arithmetic and copies ran while one was open for 7% of the time, Pallas kernels for 0%

commit v1 on v0

--- a/solution.py
+++ b/solution.py
@@ -1,8 +1,11 @@
+import functools
 import math
 
 import jax
 import jax.numpy as jnp
 from jax import lax
+from jax.experimental import pallas as pl
+from jax.experimental.pallas import tpu as pltpu
 from jax.sharding import PartitionSpec as P
 
 QUERY_HEADS = 40
@@ -10,7 +13,165 @@
 HEAD_SIZE = 128
 
 
-def local(queries, keys, values, positions, out_weight):
+def attend_kernel(qpos_ref, kpos_ref, q_ref, *refs, group, slots):
+    k_refs, v_refs, o_ref = refs[:slots], refs[slots : 2 * slots], refs[2 * slots]
+    rows = q_ref.shape[0]
+    heads = [q_ref[:, h * HEAD_SIZE : (h + 1) * HEAD_SIZE] for h in range(group)]
+    query = jnp.concatenate(heads, axis=0)
+    scale = HEAD_SIZE ** (-0.5)
+    query_pos = qpos_ref[...]
+    scores = []
+    for i in range(slots):
+        part = lax.dot_general(
+            query, k_refs[i][...], (((1,), (1,)), ((), ())), preferred_element_type=jnp.float32
+        )
+        count = part.shape[1]
+        keep = kpos_ref[:, i * count : (i + 1) * count] <= query_pos
+        part = part.reshape(group, rows, count) * scale
+        scores.append(jnp.where(keep[None], part, -1e30))
+    top = functools.reduce(jnp.maximum, [jnp.max(s, axis=-1, keepdims=True) for s in scores])
+    total = 0.0
+    accum = 0.0
+    for i in range(slots):
+        expo = jnp.exp(scores[i] - top)
+        total = total + jnp.sum(expo, axis=-1, keepdims=True)
+        weights = expo.astype(jnp.bfloat16).reshape(group * rows, -1)
+        accum = accum + jnp.dot(weights, v_refs[i][...], preferred_element_type=jnp.float32)
+    result = (accum.reshape(group, rows, HEAD_SIZE) / total).astype(jnp.bfloat16)
+    for h in range(group):
+        o_ref[:, h * HEAD_SIZE : (h + 1) * HEAD_SIZE] = result[h]
+
+
+def attend(queries, kv_slots, query_pos, key_pos):
+    tok, width = queries.shape
+    count = kv_slots[0].shape[0]
+    kv_heads = kv_slots[0].shape[1] // (2 * HEAD_SIZE)
+    group = width // (kv_heads * HEAD_SIZE)
+    slots = len(kv_slots)
+    k_spec = pl.BlockSpec((count, HEAD_SIZE), lambda g: (0, g))
+    v_spec = pl.BlockSpec((count, HEAD_SIZE), lambda g: (0, kv_heads + g))
+    q_spec = pl.BlockSpec((tok, group * HEAD_SIZE), lambda g: (0, g))
+    pairs = tok * count * slots * kv_heads * group
+    return pl.pallas_call(
+        functools.partial(attend_kernel, group=group, slots=slots),
+        out_shape=jax.ShapeDtypeStruct((tok, width), jnp.bfloat16),
+        grid=(kv_heads,),
+        in_specs=[
+            pl.BlockSpec((tok, 1), lambda g: (0, 0)),
+            pl.BlockSpec((1, slots * count), lambda g: (0, 0)),
+            q_spec,
+        ]
+        + [k_spec] * slots
+        + [v_spec] * slots,
+        out_specs=q_spec,
+        cost_estimate=pl.CostEstimate(
+            flops=4 * pairs * HEAD_SIZE, bytes_accessed=4 * tok * width, transcendentals=pairs
+        ),
+        name="attend",
+    )(query_pos.reshape(tok, 1), key_pos.reshape(1, -1), queries, *kv_slots, *kv_slots)
+
+
+def project_kernel(a_ref, b_ref, wa_ref, wb_ref, o_ref):
+    accum = jnp.dot(a_ref[...], wa_ref[...], preferred_element_type=jnp.float32)
+    accum = accum + jnp.dot(b_ref[...], wb_ref[...], preferred_element_type=jnp.float32)
+    o_ref[...] = accum.astype(jnp.bfloat16)
+
+
+def project(a, b, wa, wb, tile=256):
+    rows, depth = a.shape
+    cols = wa.shape[1]
+    a_spec = pl.BlockSpec((rows, depth), lambda n: (0, 0))
+    w_spec = pl.BlockSpec((depth, tile), lambda n: (0, n))
+    return pl.pallas_call(
+        project_kernel,
+        out_shape=jax.ShapeDtypeStruct((rows, cols), jnp.bfloat16),
+        grid=(cols // tile,),
+        in_specs=[a_spec, a_spec, w_spec, w_spec],
+        out_specs=pl.BlockSpec((rows, tile), lambda n: (0, n)),
+        cost_estimate=pl.CostEstimate(
+            flops=4 * rows * depth * cols, bytes_accessed=4 * depth * cols, transcendentals=0
+        ),
+        name="project",
+    )(a, b, wa, wb)
+
+
+FIRST = [(0, 1), (1, 0), (2, 3), (3, 2)]
+MIDDLE = [(1, 2), (2, 1)]
+OUTWARD = [(1, 0), (2, 3)]
+
+
+def xor(step):
+    return [(i, i ^ step) for i in range(4)]
+
+
+def line_gather(block, middle):
+    near = lax.ppermute(block, "ctx", FIRST)
+    across = lax.ppermute(block, "ctx", MIDDLE)
+    far = lax.ppermute(near, "ctx", MIDDLE)
+    out_near = lax.ppermute(across, "ctx", OUTWARD)
+    out_far = lax.ppermute(far, "ctx", OUTWARD)
+    third = jnp.where(middle, across, out_near)
+    fourth = jnp.where(middle, far, out_far)
+    return near, third, fourth
+
+
+def four_planes(queries, keys, values, positions, out_weight):
+    tok = queries.shape[0]
+    half = tok // 2
+    c = lax.axis_index("ctx")
+    t = lax.axis_index("tp")
+    core = t % 2
+    middle = (c == 1) | (c == 2)
+    other = jnp.where(c < 2, 2, 1)
+    order = [c, c ^ 1, other, other ^ 1]
+
+    kv = jnp.concatenate([keys, values], axis=1)
+    kv_slots = (kv,) + line_gather(kv, middle)
+    pos_of = [lax.dynamic_slice_in_dim(positions, i * tok, tok) for i in order]
+    attended = attend(queries, kv_slots, pos_of[0], jnp.concatenate(pos_of))
+
+    weight_pair = lax.ppermute(out_weight, "tp", xor(1))
+    mine = lax.dynamic_slice_in_dim(attended, core * half, half)
+    theirs = lax.dynamic_slice_in_dim(attended, (1 - core) * half, half)
+    given = lax.ppermute(theirs, "tp", xor(1))
+    block = jnp.concatenate([mine, given], axis=0)
+
+    near, third, fourth = line_gather(block, middle)
+
+    def projected(parts):
+        a = jnp.concatenate([p[:half] for p in parts], axis=0)
+        b = jnp.concatenate([p[half:] for p in parts], axis=0)
+        return project(a, b, out_weight, weight_pair)
+
+    early = projected([block, near])
+    late = projected([third, fourth])
+    own, to_near = early[:half], early[half:]
+    to_third, to_fourth = late[:half], late[half:]
+    two = jnp.where(middle, to_fourth, to_third)
+    three = jnp.where(middle, to_third, to_fourth)
+    from_one = lax.ppermute(to_near, "ctx", xor(1))
+    from_two = lax.ppermute(two, "ctx", xor(2))
+    from_three = lax.ppermute(three, "ctx", xor(3))
+    by_step = [own, from_one, from_two, from_three]
+
+    def columns(p):
+        step = p ^ c
+        return jnp.where(
+            step < 2,
+            jnp.where(step == 0, by_step[0], by_step[1]),
+            jnp.where(step == 2, by_step[2], by_step[3]),
+        )
+
+    got = [columns(t)] + [lax.ppermute(columns(t ^ j), "tp", xor(j)) for j in (1, 2, 3)]
+    f32 = jnp.float32
+    same = (got[0].astype(f32) + got[2].astype(f32)).astype(jnp.bfloat16)
+    swap = (got[1].astype(f32) + got[3].astype(f32)).astype(jnp.bfloat16)
+    top = jnp.where(core == 0, same, swap)
+    low = jnp.where(core == 0, swap, same)
+    return jnp.concatenate([top, low], axis=0)
+
+
+def any_mesh(queries, keys, values, positions, out_weight):
     tok = queries.shape[0]
     kv_heads = keys.shape[1] // HEAD_SIZE
     query_group = QUERY_HEADS // KEY_VALUE_HEADS
@@ -19,7 +180,7 @@
     query_pos = lax.dynamic_slice_in_dim(positions, ctx_index * tok, tok)
     query_four = queries.reshape(tok, kv_heads, query_group, HEAD_SIZE)
 
-    def attend(carry, key_block, value_block, key_pos):
+    def attend_block(carry, key_block, value_block, key_pos):
         top, total, accum = carry
         count = key_block.shape[0]
         key_three = key_block.reshape(count, kv_heads, HEAD_SIZE)
@@ -53,7 +214,7 @@
         key_block = lax.dynamic_slice_in_dim(key_piece, offset, width, 0)
         value_block = lax.dynamic_slice_in_dim(value_piece, offset, width, 0)
         key_pos = lax.dynamic_slice_in_dim(positions, offset, width, 0)
-        return attend(state, key_block, value_block, key_pos)
+        return attend_block(state, key_block, value_block, key_pos)
 
     top, total, accum = lax.fori_loop(0, rows // width, step, (start_top, start_total, start_accum))
     attended = (
@@ -67,15 +228,15 @@
         lax.all_gather(out_weight, "ctx", axis=1, tiled=True),
         preferred_element_type=jnp.float32,
     )
-    summed = lax.psum_scatter(
+    return lax.psum_scatter(
         partial_value.astype(jnp.bfloat16), "tp", scatter_dimension=1, tiled=True
     )
-    return summed
 
 
 def solution(mesh):
+    square = mesh.shape["ctx"] == 4 and mesh.shape["tp"] == 4
     return jax.shard_map(
-        local,
+        four_planes if square else any_mesh,
         mesh=mesh,
         in_specs=(
             P(("groups", "ctx"), "tp"),

time: 297 us -> 152 us (0.51)
  waiting for transfers between devices: 201 us -> 95.4 us
  blocking collectives: 49.9 us -> 0 us
  Pallas kernels: 0 us -> 21.7 us
  matrix products: 20.8 us -> 0 us
  starting transfers between devices: 0.04 us -> 17.2 us
  between operations: 13.5 us -> 0.23 us
  local copies, waits for them, and re-layouts: 2.89 us -> 7.47 us
    all_gather x1 -> x0, waiting for transfers between devices: 167 us -> none  [local(): lax.all_gather(out_weight, 'ctx', axis=1, tiled=True)]
    ppermute x0 -> x18, waiting for transfers between devices: none -> 95.4 us  [the longest x2 21.5 us: line_gather(): near = lax.ppermute(block, 'ctx', FIRST)]
    all_gather x2 -> x0, blocking collectives: 49.9 us -> none  [the longest x1 30.9 us: local(): key_piece = lax.all_gather(keys, 'ctx', axis=0, tiled=True)]
    reduce_scatter x1 -> x0, waiting for transfers between devices: 33.3 us -> none  [local(): lax.psum_scatter(partial_value.astype(jnp.bfloat16), 'tp', scatter_dimens...]
    pallas_call x0 -> x3, Pallas kernels: none -> 21.7 us  [the longest x2 13.3 us: project(): pl.pallas_call(project_kernel, out_shape=jax.ShapeDtypeStruct((rows, cols...]
    dot_general x5 -> x0, matrix products: 20.8 us -> none  [the longest x1 9.69 us: local(): jnp.dot(attended, lax.all_gather(out_weight, 'ctx', axis=1, tiled=True),...]
    ppermute x0 -> x18, starting transfers between devices: none -> 17.2 us  [the longest x2 3.19 us: line_gather(): near = lax.ppermute(block, 'ctx', FIRST)]
    reduce_sum x2 -> x0, other arithmetic: 7.85 us -> none  [attend(): total = total * factor + jnp.sum(expo, axis=-1)]
  transfers between devices with their start and end apart: 2 -> 18, of which waited for: 2 -> 11; matrix products, arithmetic and copies ran while one was open for 7% -> 4% of each run, Pallas kernels for 0% -> 4%
where the time goes in v1:
time: 152 us; the launch traced here: 151 us
  waiting for transfers between devices  95.4 us (63%)
  Pallas kernels  21.7 us (14%)
  starting transfers between devices  17.2 us (11%)
  other arithmetic  9.06 us (6%)
  local copies, waits for them, and re-layouts  7.47 us (5%)
    ppermute x2, waiting for transfers between devices, line_gather(): near = lax.ppermute(block, 'ctx', FIRST)  21.5 us
    ppermute x2, waiting for transfers between devices, line_gather(): out_near = lax.ppermute(across, 'ctx', OUTWARD)  21.1 us
    ppermute x2, waiting for transfers between devices, line_gather(): out_far = lax.ppermute(far, 'ctx', OUTWARD)  18.5 us
    ppermute x3, waiting for transfers between devices, four_planes(): lax.ppermute(columns(t ^ j), 'tp', xor(j))  15 us
    pallas_call x2, Pallas kernels, project(): pl.pallas_call(project_kernel, out_shape=jax.ShapeDtypeStruct((rows, cols...  13.3 us
    ppermute x1, waiting for transfers between devices, four_planes(): from_two = lax.ppermute(two, 'ctx', xor(2))  11.1 us
    pallas_call x1, Pallas kernels, attend(): pl.pallas_call(functools.partial(attend_kernel, group=group, slots=slots)...  8.37 us
    ppermute x1, waiting for transfers between devices, four_planes(): from_one = lax.ppermute(to_near, 'ctx', xor(1))  6.69 us
  transfers between devices with their start and end apart: 18, of which 11 were waited for; matrix products, arithmetic and copies ran while one was open for 4% of the time, Pallas kernels for 4%

profile of v1, /device:TPU:0, one launch (start us, length us, event | category | flops | bytes accessed | tf_op | source)
XLA Modules:
  0.0 151.0 jit_solution(11220726047617805709)
XLA Ops:
  0.9 0.9 constant_dynamic-update-slice_fusion.refs_0_.refs_4_
  1.8 3.1 %collective-permute-start = (bf16[256,512]{1,0:T(8,128)(2,1)S(1)}, bf16[256,512]{1,0:T(8,128)(2,1)S(1)}, u32[]{:S(2)}, u32[]{:S(2)}) collective-permute-start(bf16[256,512]{1,0:T(8,128)(2,1)S(1)} %constant_dynamic-update-slice_fusion.refs_0_.refs_4_), channel_id=1, source_target_pairs={{0,4},{4,0},{8,12},{12,8},{1,5},{5,1},{9,13},{13,9},{2,6},{6,2},{1... | collective-permute-start | bytes 786440 | tf_op jit(solution)/shard_map/ppermute | solution.py:108
  5.6 5.6 %collective-permute-done.refs_1_.refs_5_ = bf16[256,512]{1,0:T(8,128)(2,1)S(1)} collective-permute-done((bf16[256,512]{1,0:T(8,128)(2,1)S(1)}, bf16[256,512]{1,0:T(8,128)(2,1)S(1)}, u32[]{:S(2)}, u32[]{:S(2)}) %collective-permute-start) | collective-permute-done | bytes 262176 | tf_op jit(solution)/shard_map/ppermute | solution.py:108
  12.0 1.3 collective-permute-start.2
  13.3 0.9 fusion.3
  14.2 1.3 collective-permute-start.4
  16.9 6.7 %collective-permute-done.2 = bf16[256,512]{1,0:T(8,128)(2,1)S(1)} collective-permute-done((bf16[256,512]{1,0:T(8,128)(2,1)S(1)}, bf16[256,512]{1,0:T(8,128)(2,1)S(1)}, u32[]{:S(2)}, u32[]{:S(2)}) %collective-permute-start.2) | collective-permute-done | bytes 262176 | tf_op jit(solution)/shard_map/ppermute | solution.py:111
  24.3 4.3 %collective-permute-done.4 = bf16[256,512]{1,0:T(8,128)(2,1)S(1)} collective-permute-done((bf16[256,512]{1,0:T(8,128)(2,1)S(1)}, bf16[256,512]{1,0:T(8,128)(2,1)S(1)}, u32[]{:S(2)}, u32[]{:S(2)}) %collective-permute-start.4) | collective-permute-done | bytes 262176 | tf_op jit(solution)/shard_map/ppermute | solution.py:112
  29.3 8.4 %attend.1 = bf16[256,1280]{1,0:T(8,128)(2,1)} custom-call(s32[256,1]{1,0:T(8,128)} %copy.6.qpos_ref, s32[1,1024]{1,0:T(1,128)} %bitcast.3, bf16[256,1280]{1,0:T(8,128)(2,1)} %q_ref.1, bf16[256,512]{1,0:T(8,128)(2,1)} %copy-done.3, bf16[256,512]{1,0:T(8,128)(2,1)} %copy-done.4, bf16[256,512]{1,0:T(8,128)(2,1)} %broadcast_select_fusion.7.refs_2_.refs_6_, ...), custom_call_target="tpu_custom_call" | custom-call | flops 1342177280 | bytes 1310720 | tf_op jit(solution)/shard_map/attend/pallas_call | solution.py:55
  37.7 1.1 constant_dynamic-slice_fusion
  38.9 1.6 %collective-permute-done.5 = bf16[128,1280]{1,0:T(8,128)(2,1)S(1)} collective-permute-done((bf16[128,1280]{1,0:T(8,128)(2,1)S(1)}, bf16[128,1280]{1,0:T(8,128)(2,1)S(1)}, u32[]{:S(2)}, u32[]{:S(2)}) %collective-permute-start.5) | collective-permute-done | bytes 327712 | tf_op jit(solution)/shard_map/ppermute | solution.py:136
  41.6 15.8 %collective-permute-done.6 = bf16[256,1280]{1,0:T(8,128)(2,1)S(1)} collective-permute-done((bf16[256,1280]{1,0:T(8,128)(2,1)S(1)}, bf16[256,1280]{1,0:T(8,128)(2,1)S(1)}, u32[]{:S(2)}, u32[]{:S(2)}) %collective-permute-start.6) | collective-permute-done | bytes 655392 | tf_op jit(solution)/shard_map/ppermute | solution.py:108
  58.1 1.3 collective-permute-start.10
  59.5 1.2 pad_maximum_fusion.1
  60.6 1.3 collective-permute-start.12
  61.9 14.4 %collective-permute-done.10 = bf16[256,1280]{1,0:T(8,128)(2,1)S(1)} collective-permute-done((bf16[256,1280]{1,0:T(8,128)(2,1)S(1)}, bf16[256,1280]{1,0:T(8,128)(2,1)S(1)}, u32[]{:S(2)}, u32[]{:S(2)}) %collective-permute-start.10) | collective-permute-done | bytes 655392 | tf_op jit(solution)/shard_map/ppermute | solution.py:111
  76.4 14.2 %collective-permute-done.12 = bf16[256,1280]{1,0:T(8,128)(2,1)S(1)} collective-permute-done((bf16[256,1280]{1,0:T(8,128)(2,1)S(1)}, bf16[256,1280]{1,0:T(8,128)(2,1)S(1)}, u32[]{:S(2)}, u32[]{:S(2)}) %collective-permute-start.12) | collective-permute-done | bytes 655392 | tf_op jit(solution)/shard_map/ppermute | solution.py:112
  90.7 1.2 pad_maximum_fusion.3
  91.9 1.7 %copy-done.1 = bf16[1280,1280]{1,0:T(8,128)(2,1)} copy-done((bf16[1280,1280]{1,0:T(8,128)(2,1)}, bf16[1280,1280]{1,0:T(8,128)(2,1)S(1)}, u32[]{:S(2)}) %copy-start.1) | copy-done | bytes 3276824
  93.6 6.7 %project.3 = bf16[256,1280]{1,0:T(8,128)(2,1)} custom-call(bf16[256,1280]{1,0:T(8,128)(2,1)} %get-tuple-element.24.a_ref, bf16[256,1280]{1,0:T(8,128)(2,1)} %get-tuple-element.25.b_ref, bf16[1280,1280]{1,0:T(8,128)(2,1)} %wa_ref.3, bf16[1280,1280]{1,0:T(8,128)(2,1)} %copy-done.1), custom_call_target="tpu_custom_call" | custom-call | flops 1677721600 | bytes 6553600 | tf_op jit(solution)/shard_map/project/pallas_call | solution.py:85
  100.2 1.1 broadcast_select_fusion.2
  101.7 2.0 %collective-permute-start.14 = (bf16[128,1280]{1,0:T(8,128)(2,1)S(1)}, bf16[128,1280]{1,0:T(8,128)(2,1)S(1)}, u32[]{:S(2)}, u32[]{:S(2)}) collective-permute-start(bf16[128,1280]{1,0:T(8,128)(2,1)S(1)} %get-tuple-element.12), channel_id=1, source_target_pairs={{0,12},{4,8},{8,4},{12,0},{1,13},{5,9},{9,5},{13,1},{2,14},{6,10},... | collective-permute-start | bytes 983048 | tf_op jit(solution)/shard_map/ppermute | solution.py:154
  103.7 6.6 %project.2 = bf16[256,1280]{1,0:T(8,128)(2,1)} custom-call(bf16[256,1280]{1,0:T(8,128)(2,1)} %get-tuple-element.26.a_ref, bf16[256,1280]{1,0:T(8,128)(2,1)} %get-tuple-element.27.b_ref, bf16[1280,1280]{1,0:T(8,128)(2,1)} %wa_ref.3, bf16[1280,1280]{1,0:T(8,128)(2,1)} %copy-done.1), custom_call_target="tpu_custom_call" | custom-call | flops 1677721600 | bytes 6553600 | tf_op jit(solution)/shard_map/project/pallas_call | solution.py:85
  110.3 1.0 slice.43
  111.3 1.3 collective-permute-start.8
  112.6 11.1 %collective-permute-done.13 = bf16[128,1280]{1,0:T(8,128)(2,1)S(1)} collective-permute-done((bf16[128,1280]{1,0:T(8,128)(2,1)S(1)}, bf16[128,1280]{1,0:T(8,128)(2,1)S(1)}, u32[]{:S(2)}, u32[]{:S(2)}) %collective-permute-start.13) | collective-permute-done | bytes 327712 | tf_op jit(solution)/shard_map/ppermute | solution.py:153
  123.8 6.7 %collective-permute-done.8 = bf16[128,1280]{1,0:T(8,128)(2,1)S(1)} collective-permute-done((bf16[128,1280]{1,0:T(8,128)(2,1)S(1)}, bf16[128,1280]{1,0:T(8,128)(2,1)S(1)}, u32[]{:S(2)}, u32[]{:S(2)}) %collective-permute-start.8) | collective-permute-done | bytes 327712 | tf_op jit(solution)/shard_map/ppermute | solution.py:152
  130.5 1.1 select_select_fusion.2
  131.5 1.0 collective-permute-start.17
  133.7 7.8 %collective-permute-done.17 = bf16[128,1280]{1,0:T(8,128)(2,1)S(1)} collective-permute-done((bf16[128,1280]{1,0:T(8,128)(2,1)S(1)}, bf16[128,1280]{1,0:T(8,128)(2,1)S(1)}, u32[]{:S(2)}, u32[]{:S(2)}) %collective-permute-start.17) | collective-permute-done | bytes 327712 | tf_op jit(solution)/shard_map/ppermute | solution.py:165
  141.6 7.2 %collective-permute-done.15 = bf16[128,1280]{1,0:T(8,128)(2,1)} collective-permute-done((bf16[128,1280]{1,0:T(8,128)(2,1)S(1)}, bf16[128,1280]{1,0:T(8,128)(2,1)}, u32[]{:S(2)}, u32[]{:S(2)}) %collective-permute-start.15) | collective-permute-done | bytes 327712 | tf_op jit(solution)/shard_map/ppermute | solution.py:165
  148.7 1.3 broadcast_select_fusion.5
  (39 shorter events, 9.7 us)
Async XLA Ops:
  1.8 27.5 %copy-start.3 = (bf16[256,512]{1,0:T(8,128)(2,1)}, bf16[256,512]{1,0:T(8,128)(2,1)S(1)}, u32[]{:S(2)}) copy-start(bf16[256,512]{1,0:T(8,128)(2,1)S(1)} %constant_dynamic-update-slice_fusion.refs_0_.refs_4_) | copy-start | bytes 786436
  1.8 9.4 %collective-permute-start = (bf16[256,512]{1,0:T(8,128)(2,1)S(1)}, bf16[256,512]{1,0:T(8,128)(2,1)S(1)}, u32[]{:S(2)}, u32[]{:S(2)}) collective-permute-start(bf16[256,512]{1,0:T(8,128)(2,1)S(1)} %constant_dynamic-update-slice_fusion.refs_0_.refs_4_), channel_id=1, source_target_pairs={{0,4},{4,0},{8,12},{12,8},{1,5},{5,1},{9,13},{13,9},{2,6},{6,2},{1... | collective-permute-start | bytes 786440 | tf_op jit(solution)/shard_map/ppermute | solution.py:108
  5.0 7.0 %collective-permute-start.1 = (bf16[256,512]{1,0:T(8,128)(2,1)S(1)}, bf16[256,512]{1,0:T(8,128)(2,1)S(1)}, u32[]{:S(2)}, u32[]{:S(2)}) collective-permute-start(bf16[256,512]{1,0:T(8,128)(2,1)S(1)} %constant_dynamic-update-slice_fusion.refs_0_.refs_4_), channel_id=1, source_target_pairs={{4,8},{8,4},{5,9},{9,5},{6,10},{10,6},{7,11},{11,7},{20,24},{24,20... | collective-permute-start | bytes 786440 | tf_op jit(solution)/shard_map/ppermute | solution.py:109
  11.3 2.9 %copy-start.4 = (bf16[256,512]{1,0:T(8,128)(2,1)}, bf16[256,512]{1,0:T(8,128)(2,1)S(1)}, u32[]{:S(2)}) copy-start(bf16[256,512]{1,0:T(8,128)(2,1)S(1)} %collective-permute-done.refs_1_.refs_5_) | copy-start | bytes 786436
  11.3 2.9 %collective-permute-start.3 = (bf16[256,512]{1,0:T(8,128)(2,1)S(1)}, bf16[256,512]{1,0:T(8,128)(2,1)S(1)}, u32[]{:S(2)}, u32[]{:S(2)}) collective-permute-start(bf16[256,512]{1,0:T(8,128)(2,1)S(1)} %collective-permute-done.refs_1_.refs_5_), channel_id=1, source_target_pairs={{4,8},{8,4},{5,9},{9,5},{6,10},{10,6},{7,11},{11,7},{20,24},{24,20... | collective-permute-start | bytes 786440 | tf_op jit(solution)/shard_map/ppermute | solution.py:110
  12.0 11.6 %collective-permute-start.2 = (bf16[256,512]{1,0:T(8,128)(2,1)S(1)}, bf16[256,512]{1,0:T(8,128)(2,1)S(1)}, u32[]{:S(2)}, u32[]{:S(2)}) collective-permute-start(bf16[256,512]{1,0:T(8,128)(2,1)S(1)} %collective-permute-done.1), channel_id=1, source_target_pairs={{4,0},{8,12},{5,1},{9,13},{6,2},{10,14},{7,3},{11,15},{20,16},{24,... | collective-permute-start | bytes 786440 | tf_op jit(solution)/shard_map/ppermute | solution.py:111
  14.2 14.4 %collective-permute-start.4 = (bf16[256,512]{1,0:T(8,128)(2,1)S(1)}, bf16[256,512]{1,0:T(8,128)(2,1)S(1)}, u32[]{:S(2)}, u32[]{:S(2)}) collective-permute-start(bf16[256,512]{1,0:T(8,128)(2,1)S(1)} %collective-permute-done.3), channel_id=1, source_target_pairs={{4,0},{8,12},{5,1},{9,13},{6,2},{10,14},{7,3},{11,15},{20,16},{24,... | collective-permute-start | bytes 786440 | tf_op jit(solution)/shard_map/ppermute | solution.py:112
  29.3 12.0 %copy-start = (bf16[1280,1280]{1,0:T(8,128)(2,1)S(1)}, bf16[1280,1280]{1,0:T(8,128)(2,1)}, u32[]{:S(2)}) copy-start(bf16[1280,1280]{1,0:T(8,128)(2,1)} %wa_ref.3) | copy-start | bytes 9830404
  38.8 1.7 %collective-permute-start.5 = (bf16[128,1280]{1,0:T(8,128)(2,1)S(1)}, bf16[128,1280]{1,0:T(8,128)(2,1)S(1)}, u32[]{:S(2)}, u32[]{:S(2)}) collective-permute-start(bf16[128,1280]{1,0:T(8,128)(2,1)S(1)} %get-tuple-element.18), channel_id=1, source_target_pairs={{0,1},{1,0},{2,3},{3,2},{4,5},{5,4},{6,7},{7,6},{8,9},{9,8},{10,11... | collective-permute-start | bytes 983048 | tf_op jit(solution)/shard_map/ppermute | solution.py:136
  40.6 16.8 %collective-permute-start.6 = (bf16[256,1280]{1,0:T(8,128)(2,1)S(1)}, bf16[256,1280]{1,0:T(8,128)(2,1)S(1)}, u32[]{:S(2)}, u32[]{:S(2)}) collective-permute-start(bf16[256,1280]{1,0:T(8,128)(2,1)S(1)} %pad_maximum_fusion), channel_id=1, source_target_pairs={{0,4},{4,0},{8,12},{12,8},{1,5},{5,1},{9,13},{13,9},{2,6},{6,2},{1... | collective-permute-start | bytes 1966088 | tf_op jit(solution)/shard_map/ppermute | solution.py:108
  40.6 17.5 %collective-permute-start.9 = (bf16[256,1280]{1,0:T(8,128)(2,1)S(1)}, bf16[256,1280]{1,0:T(8,128)(2,1)S(1)}, u32[]{:S(2)}, u32[]{:S(2)}) collective-permute-start(bf16[256,1280]{1,0:T(8,128)(2,1)S(1)} %pad_maximum_fusion), channel_id=1, source_target_pairs={{4,8},{8,4},{5,9},{9,5},{6,10},{10,6},{7,11},{11,7},{20,24},{24,20... | collective-permute-start | bytes 1966088 | tf_op jit(solution)/shard_map/ppermute | solution.py:109
  41.4 50.6 %collective-permute-start.7 = (bf16[1280,1280]{1,0:T(8,128)(2,1)S(1)}, bf16[1280,1280]{1,0:T(8,128)(2,1)S(1)}, u32[]{:S(2)}, u32[]{:S(2)}) collective-permute-start(bf16[1280,1280]{1,0:T(8,128)(2,1)S(1)} %copy-done), channel_id=1, source_target_pairs={{0,1},{1,0},{2,3},{3,2},{4,5},{5,4},{6,7},{7,6},{8,9},{9,8},{10,11... | collective-permute-start | bytes 9830408 | tf_op jit(solution)/shard_map/ppermute | solution.py:133
  57.4 3.2 %collective-permute-start.11 = (bf16[256,1280]{1,0:T(8,128)(2,1)S(1)}, bf16[256,1280]{1,0:T(8,128)(2,1)S(1)}, u32[]{:S(2)}, u32[]{:S(2)}) collective-permute-start(bf16[256,1280]{1,0:T(8,128)(2,1)S(1)} %collective-permute-done.6), channel_id=1, source_target_pairs={{4,8},{8,4},{5,9},{9,5},{6,10},{10,6},{7,11},{11,7},{20,24},{24,20... | collective-permute-start | bytes 1966088 | tf_op jit(solution)/shard_map/ppermute | solution.py:110
  58.1 18.2 %collective-permute-start.10 = (bf16[256,1280]{1,0:T(8,128)(2,1)S(1)}, bf16[256,1280]{1,0:T(8,128)(2,1)S(1)}, u32[]{:S(2)}, u32[]{:S(2)}) collective-permute-start(bf16[256,1280]{1,0:T(8,128)(2,1)S(1)} %collective-permute-done.9), channel_id=1, source_target_pairs={{4,0},{8,12},{5,1},{9,13},{6,2},{10,14},{7,3},{11,15},{20,16},{24,... | collective-permute-start | bytes 1966088 | tf_op jit(solution)/shard_map/ppermute | solution.py:111
  60.6 30.0 %collective-permute-start.12 = (bf16[256,1280]{1,0:T(8,128)(2,1)S(1)}, bf16[256,1280]{1,0:T(8,128)(2,1)S(1)}, u32[]{:S(2)}, u32[]{:S(2)}) collective-permute-start(bf16[256,1280]{1,0:T(8,128)(2,1)S(1)} %collective-permute-done.11), channel_id=1, source_target_pairs={{4,0},{8,12},{5,1},{9,13},{6,2},{10,14},{7,3},{11,15},{20,16},{24,... | collective-permute-start | bytes 1966088 | tf_op jit(solution)/shard_map/ppermute | solution.py:112
  91.9 1.7 %copy-start.1 = (bf16[1280,1280]{1,0:T(8,128)(2,1)}, bf16[1280,1280]{1,0:T(8,128)(2,1)S(1)}, u32[]{:S(2)}) copy-start(bf16[1280,1280]{1,0:T(8,128)(2,1)S(1)} %collective-permute-done.7.wb_ref) | copy-start | bytes 9830404
  101.4 22.4 %collective-permute-start.13 = (bf16[128,1280]{1,0:T(8,128)(2,1)S(1)}, bf16[128,1280]{1,0:T(8,128)(2,1)S(1)}, u32[]{:S(2)}, u32[]{:S(2)}) collective-permute-start(bf16[128,1280]{1,0:T(8,128)(2,1)S(1)} %get-tuple-element.13), channel_id=1, source_target_pairs={{0,8},{4,12},{8,0},{12,4},{1,9},{5,13},{9,1},{13,5},{2,10},{6,14},... | collective-permute-start | bytes 983048 | tf_op jit(solution)/shard_map/ppermute | solution.py:153
  101.7 22.1 %collective-permute-start.14 = (bf16[128,1280]{1,0:T(8,128)(2,1)S(1)}, bf16[128,1280]{1,0:T(8,128)(2,1)S(1)}, u32[]{:S(2)}, u32[]{:S(2)}) collective-permute-start(bf16[128,1280]{1,0:T(8,128)(2,1)S(1)} %get-tuple-element.12), channel_id=1, source_target_pairs={{0,12},{4,8},{8,4},{12,0},{1,13},{5,9},{9,5},{13,1},{2,14},{6,10},... | collective-permute-start | bytes 983048 | tf_op jit(solution)/shard_map/ppermute | solution.py:154
  111.3 37.5 %copy-start.2 = (bf16[256,1280]{1,0:T(8,128)(2,1)S(1)}, bf16[256,1280]{1,0:T(8,128)(2,1)}, u32[]{:S(2)}) copy-start(bf16[256,1280]{1,0:T(8,128)(2,1)} %project.2) | copy-start | bytes 1966084
  111.3 19.1 %collective-permute-start.8 = (bf16[128,1280]{1,0:T(8,128)(2,1)S(1)}, bf16[128,1280]{1,0:T(8,128)(2,1)S(1)}, u32[]{:S(2)}, u32[]{:S(2)}) collective-permute-start(bf16[128,1280]{1,0:T(8,128)(2,1)S(1)} %slice.43), channel_id=1, source_target_pairs={{0,4},{4,0},{8,12},{12,8},{1,5},{5,1},{9,13},{13,9},{2,6},{6,2},{1... | collective-permute-start | bytes 983048 | tf_op jit(solution)/shard_map/ppermute | solution.py:152
  131.5 10.0 %collective-permute-start.17 = (bf16[128,1280]{1,0:T(8,128)(2,1)S(1)}, bf16[128,1280]{1,0:T(8,128)(2,1)S(1)}, u32[]{:S(2)}, u32[]{:S(2)}) collective-permute-start(bf16[128,1280]{1,0:T(8,128)(2,1)S(1)} %get-tuple-element.8), channel_id=1, source_target_pairs={{0,3},{1,2},{2,1},{3,0},{4,7},{5,6},{6,5},{7,4},{8,11},{9,10},{10,... | collective-permute-start | bytes 983048 | tf_op jit(solution)/shard_map/ppermute | solution.py:165
  132.5 9.0 %collective-permute-start.16 = (bf16[128,1280]{1,0:T(8,128)(2,1)S(1)}, bf16[128,1280]{1,0:T(8,128)(2,1)S(1)}, u32[]{:S(2)}, u32[]{:S(2)}) collective-permute-start(bf16[128,1280]{1,0:T(8,128)(2,1)S(1)} %get-tuple-element.9), channel_id=1, source_target_pairs={{0,1},{1,0},{2,3},{3,2},{4,5},{5,4},{6,7},{7,6},{8,9},{9,8},{10,11... | collective-permute-start | bytes 983048 | tf_op jit(solution)/shard_map/ppermute | solution.py:165
  133.2 15.5 %collective-permute-start.15 = (bf16[128,1280]{1,0:T(8,128)(2,1)S(1)}, bf16[128,1280]{1,0:T(8,128)(2,1)}, u32[]{:S(2)}, u32[]{:S(2)}) collective-permute-start(bf16[128,1280]{1,0:T(8,128)(2,1)S(1)} %get-tuple-element.7), channel_id=1, source_target_pairs={{0,2},{1,3},{2,0},{3,1},{4,6},{5,7},{6,4},{7,5},{8,10},{9,11},{10,... | collective-permute-start | bytes 983048 | tf_op jit(solution)/shard_map/ppermute | solution.py:165
